TPU v7x, 512 devices: a whole 4x4x16 slice. The times are simulated.
512 devices in a mesh: seq: 32 (over y, x, core), head: 16 (over z).
Axes of the slice: x: 4, y: 4, z: 16, core: 2. Of those that a mesh axis runs over, the one named last changes fastest.
Arguments:
- queries: bfloat16 [16384, 8192], P('seq', 'head'), may hold values from -0.9 to 0.9
- keys: bfloat16 [16384, 8192], P('seq', 'head'), may hold values from -0.9 to 0.9
- values: bfloat16 [16384, 8192], P('seq', 'head'), may hold values from -0.9 to 0.9
- grad_out: bfloat16 [16384, 8192], P('seq', 'head'), may hold values from -0.9 to 0.9
- rates: float32 [64], P('head'), may hold values from 3.0517578e-05 to 0.04
- doc_lengths: int32 [8], replicated, may hold values from 1 to 12288, 16384 in all
Outputs:
- grad_queries: bfloat16 [16384, 8192], P(('seq', 'head'))
- grad_keys: bfloat16 [16384, 8192], P(('seq', 'head'))
- grad_values: bfloat16 [16384, 8192], P(('seq', 'head'))
Inputs may be any that keep to these rules, and one draw needn't show every extreme that they name: `doc_lengths`: lengths of the completions in order, summing to 16384; the longest has exactly 12288 tokens.
All inputs are finite; a program needn't handle non-finite values.
Results may differ from a plain program's by a relative error of at most 0.001.
The roundings to bfloat16 on the way count: a program that leaves them out, or rounds other values in their place, can miss the bound.
Values may be sent and summed in bfloat16 or wider, within the bound.
No kernel may reach another device: no remote copies, remote signals or barrier semaphores. Data moves between devices by JAX's collectives and lax.ppermute only.
A program may use at most 64 MiB of HBM per device.

v0:
```python
import jax
import jax.numpy as jnp
from jax import lax
from jax.sharding import PartitionSpec as P


def sent_together(arrays, axis, dim, along):
    widths = [a.shape[along] for a in arrays]
    both = jnp.concatenate(arrays, axis=along)
    filled = lax.all_gather(both, axis, axis=dim, tiled=True)
    return tuple(jnp.split(filled, [sum(widths[:k]) for k in range(1, len(widths))], axis=along))


def seg_ids(doc_lengths, positions):
    starts = jnp.cumsum(doc_lengths, dtype=jnp.int32) - doc_lengths
    inside = (starts[None, :] <= positions[:, None]).astype(jnp.int32)
    return jnp.sum(inside, axis=1, dtype=jnp.int32) - 1


def body(queries, keys, values, grad_out, rates, doc_lengths):
    length = queries.shape[0]
    heads_here = rates.shape[0]
    head_dim = queries.shape[1] // heads_here
    query_rows = queries.reshape(length, heads_here, head_dim)
    key_rows = keys.reshape(length, heads_here, head_dim)
    value_rows = values.reshape(length, heads_here, head_dim)
    grad_rows = grad_out.reshape(length, heads_here, head_dim)
    shard = lax.axis_index("seq")
    shards = lax.axis_size("seq")
    first_pos = shard * length
    positions = first_pos + jnp.arange(length, dtype=jnp.int32)
    segment = seg_ids(doc_lengths, positions)
    edges = seg_ids(doc_lengths, jnp.stack([first_pos - 1, first_pos + length]))
    seg_prev = edges[0]
    seg_next = edges[1]
    offsets = jnp.arange(length, dtype=jnp.float32)
    weight_k = jnp.where(
        (segment == segment[-1])[:, None],
        jnp.exp(-rates[None, :] * (length - 1.0 - offsets)[:, None]),
        0.0,
    )
    weighted_k = (key_rows.astype(jnp.float32) * weight_k[:, :, None]).astype(jnp.bfloat16)
    summary_fwd = jnp.einsum(
        "uhd,uhe->hde", weighted_k, value_rows, preferred_element_type=jnp.float32
    )
    weight_q = jnp.where(
        (segment == segment[0])[:, None], jnp.exp(-rates[None, :] * offsets[:, None]), 0.0
    )
    weighted_q = (query_rows.astype(jnp.float32) * weight_q[:, :, None]).astype(jnp.bfloat16)
    summary_bwd = jnp.einsum(
        "thd,the->hde", weighted_q, grad_rows, preferred_element_type=jnp.float32
    )
    gathered_fwd, gathered_bwd = sent_together((summary_fwd[None], summary_bwd[None]), "seq", 0, 1)
    blocks_all = jnp.arange(shards, dtype=jnp.int32)
    firsts = blocks_all * length
    breaks_fwd = (
        seg_ids(doc_lengths, firsts + length - 1) != seg_ids(doc_lengths, firsts - 1)
    ).astype(jnp.int32)
    breaks_bwd = (seg_ids(doc_lengths, firsts) != seg_ids(doc_lengths, firsts + length)).astype(
        jnp.int32
    )
    count_fwd = jnp.cumsum(breaks_fwd, dtype=jnp.int32)
    count_bwd = jnp.cumsum(breaks_bwd, dtype=jnp.int32)
    before_here = jnp.sum(jnp.where(blocks_all == shard - 1, count_fwd, 0), dtype=jnp.int32)
    valid_fwd = (blocks_all < shard) & (before_here - count_fwd == 0)
    gap_fwd = jnp.maximum(shard - 1 - blocks_all, 0).astype(jnp.float32)
    mixing_fwd = jnp.where(
        valid_fwd[:, None], jnp.exp(-rates[None, :] * length * gap_fwd[:, None]), 0.0
    )
    state_in = jnp.einsum("ih,ihde->hde", mixing_fwd, gathered_fwd, precision=lax.Precision.HIGHEST)
    here_bwd = jnp.sum(jnp.where(blocks_all == shard, count_bwd, 0), dtype=jnp.int32)
    valid_bwd = (blocks_all > shard) & (count_bwd - breaks_bwd - here_bwd == 0)
    gap_bwd = jnp.maximum(blocks_all - 1 - shard, 0).astype(jnp.float32)
    mixing_bwd = jnp.where(
        valid_bwd[:, None], jnp.exp(-rates[None, :] * length * gap_bwd[:, None]), 0.0
    )
    back_in = jnp.einsum("ih,ihde->hde", mixing_bwd, gathered_bwd, precision=lax.Precision.HIGHEST)
    distance = offsets[:, None] - offsets[None, :]
    allowed = (segment[:, None] == segment[None, :]) & (distance >= 0)
    decayed = jnp.where(
        allowed[None], jnp.exp(-rates[:, None, None] * jnp.maximum(distance, 0.0)[None]), 0.0
    )
    scores_gv = jnp.einsum(
        "the,uhe->htu", grad_rows, value_rows, preferred_element_type=jnp.float32
    )
    scores_qk = jnp.einsum("thd,uhd->htu", query_rows, key_rows, preferred_element_type=jnp.float32)
    weights_p = (decayed * scores_gv).astype(jnp.bfloat16)
    weights_a = (decayed * scores_qk).astype(jnp.bfloat16)
    local_q = jnp.einsum("htu,uhd->thd", weights_p, key_rows, preferred_element_type=jnp.float32)
    local_k = jnp.einsum("htu,thd->uhd", weights_p, query_rows, preferred_element_type=jnp.float32)
    local_v = jnp.einsum("htu,the->uhe", weights_a, grad_rows, preferred_element_type=jnp.float32)
    factor_in = jnp.where(
        (segment == seg_prev)[:, None], jnp.exp(-rates[None, :] * (offsets + 1.0)[:, None]), 0.0
    )
    factor_back = jnp.where(
        (segment == seg_next)[:, None], jnp.exp(-rates[None, :] * (length - offsets)[:, None]), 0.0
    )
    state_b = state_in.astype(jnp.bfloat16)
    back_b = back_in.astype(jnp.bfloat16)
    outer_q = (
        jnp.einsum("the,hde->thd", grad_rows, state_b, preferred_element_type=jnp.float32)
        * factor_in[:, :, None]
    )
    outer_k = (
        jnp.einsum("the,hde->thd", value_rows, back_b, preferred_element_type=jnp.float32)
        * factor_back[:, :, None]
    )
    outer_v = (
        jnp.einsum("thd,hde->the", key_rows, back_b, preferred_element_type=jnp.float32)
        * factor_back[:, :, None]
    )
    grad_q = (local_q + outer_q).astype(jnp.bfloat16).reshape(length, heads_here * head_dim)
    grad_k = (local_k + outer_k).astype(jnp.bfloat16).reshape(length, heads_here * head_dim)
    grad_v = (local_v + outer_v).astype(jnp.bfloat16).reshape(length, heads_here * head_dim)
    grad_queries, grad_keys, grad_values = (
        lax.all_to_all(grad_q, "head", split_axis=0, concat_axis=1, tiled=True),
        lax.all_to_all(grad_k, "head", split_axis=0, concat_axis=1, tiled=True),
        lax.all_to_all(grad_v, "head", split_axis=0, concat_axis=1, tiled=True),
    )
    return (grad_queries, grad_keys, grad_values)


def solution(mesh):
    return jax.shard_map(
        body,
        mesh=mesh,
        in_specs=(
            P("seq", "head"),
            P("seq", "head"),
            P("seq", "head"),
            P("seq", "head"),
            P("head"),
            P(),
        ),
        out_specs=(P(("seq", "head"), None), P(("seq", "head"), None), P(("seq", "head"), None)),
        check_vma=False,
    )
```

profile of v0, /device:TPU:2, one launch (start us, length us, event | category | flops | bytes accessed | tf_op | source)
XLA Modules:
  0.0 247.8 jit_solution(820188501126956010)
XLA Ops:
  7.2 0.0 copy-start
  7.2 0.0 all-gather.2.cloned.1.call-start
  7.3 0.9 reduce-window.23
  8.2 0.7 bitcast_subtract_fusion
  8.8 0.1 pad_add_fusion
  8.9 0.2 fusion.37
  9.1 0.6 fusion.44
  9.7 0.1 convert_reduce_fusion
  9.8 0.7 fusion.43
  10.4 0.7 broadcast_multiply_fusion
  11.1 1.3 copy.154
  12.3 0.0 copy-start.3
  12.3 1.4 copy.153
  13.8 2.5 %broadcast_compare_fusion = (pred[512]{0:T(512)(128)(4,1)S(1)}, pred[512]{0:T(512)(128)(4,1)S(1)}, pred[512]{0:T(512)(128)(4,1)S(1)}, pred[512]{0:T(512)(128)(4,1)S(1)}) fusion(s32[]{:T(128)} %bitcast.21, s32[512]{0:T(512)S(1)} %convert_reduce_fusion, s32[]{:T(128)} %bitcast.7, s32[]{:T(128)} %bitcast.9, s32[]{:T(128)} %bitcast.16), kind=kLoop, calls=%fused_computation.75 | loop fusion | flops 2560 | bytes 4112 | tf_op jit(solution)/shard_map/eq | solution.py:96
  16.4 0.1 exponential_select_fusion.1
  16.4 0.0 copy-done
  16.5 0.3 convolution_bitcast_fusion.5
  16.8 1.3 convolution_bitcast_fusion.6
  18.1 0.8 pad_maximum_fusion
  18.9 0.0 all-gather.2.cloned.1.call-update
  19.0 0.1 convert_reduce_fusion.2
  19.1 0.1 copy.122
  19.2 0.1 reduce-window.25
  19.2 0.1 reduce.2
  19.4 0.1 copy.111
  19.5 0.1 reduce-window.24
  19.5 0.1 reduce.1
  19.6 0.6 fusion.40
  20.3 0.6 fusion.38
  20.9 1.2 compare_and_fusion
  22.1 0.1 select_bitcast_fusion
  22.2 0.1 copy.136
  22.3 0.2 fusion.15
  22.5 0.0 copy-done.3
  22.5 0.3 fusion.17
  22.8 0.7 copy-done.5
  23.5 2.3 multiply_convert_fusion.1
  25.7 1.7 convolution_bitcast_fusion.1
  27.5 83.9 %all-gather.2.cloned.1.call-done = f32[32,8,128,128]{3,2,1,0:T(8,128)} async-done(((f32[1,8,128,128]{3,2,1,0:T(8,128)}), f32[32,8,128,128]{3,2,1,0:T(8,128)}) %all-gather.2.cloned.1.call-update) | async-done | bytes 16777232 | tf_op jit(solution)/shard_map/all_gather | solution.py:10
  111.4 3.4 %slice-done = f32[32,4,128,128]{3,2,1,0:T(8,128)S(1)} async-done(((f32[32,8,128,128]{3,2,1,0:T(8,128)}), f32[32,4,128,128]{3,2,1,0:T(8,128)S(1)}, s32[]{:S(2)}) %slice-start) | async-done | bytes 8388632 | tf_op jit(solution)/shard_map/split | solution.py:11
  114.8 8.8 %fusion.2 = f32[4,1,128,128]{3,1,2,0:T(1,128)S(1)} fusion(f32[32,4,1,1]{0,2,3,1:T(1,128)S(1)} %copy.136, f32[32,4,128,128]{3,2,1,0:T(8,128)S(1)} %slice-done), kind=kOutput, calls=%fused_computation.3 | convolution fusion | flops 25165824 | bytes 8651264 | tf_op jit(solution)/shard_map/ih,ihde->hde/dot_general | solution.py:70
  123.6 0.4 fusion.12
  124.0 1.2 copy.118
  125.2 2.0 all_to_all.42
  127.2 12.3 %all-to-all-start = ((bf16[16,32,512]{2,1,0:T(8,128)(2,1)}), bf16[16,32,512]{2,1,0:T(8,128)(2,1)}, u32[]{:S(2)}, u32[]{:S(2)}) async-start(bf16[16,32,512]{2,1,0:T(8,128)(2,1)} %all_to_all.42), calls=%async_computation | async-start | bytes 1048576 | tf_op jit(solution)/shard_map/all_to_all | solution.py:116
  139.5 3.0 %convolution_bitcast_fusion = f32[512,4,128]{2,0,1:T(8,128)} fusion(bf16[4,512,512]{2,1,0:T(8,128)(2,1)S(1)} %multiply_convert_fusion.1, bf16[512,4,128]{0,2,1:T(8,128)(2,1)} %bitcast.124), kind=kOutput, calls=%fused_computation.10 | convolution fusion | flops 268435456 | bytes 3670016 | tf_op jit(solution)/shard_map/htu,thd->uhd/dot_general | solution.py:90
  142.5 4.1 %fusion.1 = bf16[4,128,128]{2,1,0:T(8,128)(2,1)S(1)} fusion(f32[32,8,128,128]{3,2,1,0:T(8,128)} %all-gather.2.cloned.1.call-done, f32[4,32]{0,1:T(8,128)S(1)} %get-tuple-element.13), kind=kLoop, calls=%fused_computation.2 | loop fusion | flops 4128768 | bytes 8520192
  146.6 0.0 copy-start.4
  146.6 0.1 copy.147
  146.8 1.4 fusion.14
  148.2 0.4 copy.126
  148.6 1.0 all_to_all.46
  149.6 19.2 %all-to-all-done = bf16[16,32,512]{2,1,0:T(8,128)(2,1)} async-done(((bf16[16,32,512]{2,1,0:T(8,128)(2,1)}), bf16[16,32,512]{2,1,0:T(8,128)(2,1)}, u32[]{:S(2)}, u32[]{:S(2)}) %all-to-all-start) | async-done | bytes 524320 | tf_op jit(solution)/shard_map/all_to_all | solution.py:116
  168.8 6.6 %all-to-all-start.1 = ((bf16[16,32,512]{2,1,0:T(8,128)(2,1)}), bf16[16,32,512]{2,1,0:T(8,128)(2,1)S(1)}, u32[]{:S(2)}, u32[]{:S(2)}) async-start(bf16[16,32,512]{2,1,0:T(8,128)(2,1)} %all_to_all.46), calls=%async_computation.1 | async-start | bytes 1048576 | tf_op jit(solution)/shard_map/all_to_all | solution.py:117
  175.4 3.0 %fusion.5 = f32[512,4,128]{2,0,1:T(8,128)S(1)} fusion(bf16[512,4,128]{0,2,1:T(8,128)(2,1)S(1)} %bitcast.125, bf16[512,4,128]{0,2,1:T(8,128)(2,1)S(1)} %bitcast.121, f32[512,512]{1,0:T(8,128)} %copy-done.5, f32[4]{0:T(128)S(1)} %get-tuple-element.22, pred[512,512]{1,0:T(8,128)(4,1)S(1)} %fusion.17, bf16[512,512]{1,0:T(8,128)(2,1)S(1)} %copy-done), kind=kOutput, calls=%fused_computation.9 | convolution fusion | flops 541065216 | bytes 3932176 | tf_op jit(solution)/shard_map/htu,the->uhe/dot_general | solution.py:91
  178.4 0.5 fusion.13
  178.9 0.4 copy.134
  179.4 1.0 all_to_all.50
  180.3 24.2 %all-to-all-done.1 = bf16[16,32,512]{2,1,0:T(8,128)(2,1)S(1)} async-done(((bf16[16,32,512]{2,1,0:T(8,128)(2,1)}), bf16[16,32,512]{2,1,0:T(8,128)(2,1)S(1)}, u32[]{:S(2)}, u32[]{:S(2)}) %all-to-all-start.1) | async-done | bytes 524320 | tf_op jit(solution)/shard_map/all_to_all | solution.py:117
  204.5 6.4 %all-to-all-start.2 = ((bf16[16,32,512]{2,1,0:T(8,128)(2,1)}), bf16[16,32,512]{2,1,0:T(8,128)(2,1)S(1)}, u32[]{:S(2)}, u32[]{:S(2)}) async-start(bf16[16,32,512]{2,1,0:T(8,128)(2,1)} %all_to_all.50), calls=%async_computation.2 | async-start | bytes 1048576 | tf_op jit(solution)/shard_map/all_to_all | solution.py:118
  211.0 1.9 copy.157
  212.8 0.8 copy.158
  213.7 26.4 %all-to-all-done.2 = bf16[16,32,512]{2,1,0:T(8,128)(2,1)S(1)} async-done(((bf16[16,32,512]{2,1,0:T(8,128)(2,1)}), bf16[16,32,512]{2,1,0:T(8,128)(2,1)S(1)}, u32[]{:S(2)}, u32[]{:S(2)}) %all-to-all-start.2) | async-done | bytes 524320 | tf_op jit(solution)/shard_map/all_to_all | solution.py:118
  240.1 0.8 copy.159
  (19 shorter events, 0.1 us)
Async XLA Ops:
  7.2 9.3 %copy-start = (bf16[512,512]{1,0:T(8,128)(2,1)S(1)}, bf16[512,512]{1,0:T(8,128)(2,1)}, u32[]{:S(2)}) copy-start(bf16[512,512]{1,0:T(8,128)(2,1)} %param.9) | copy-start | bytes 1572868
  7.2 104.2 %all-gather.2.cloned.1.call-start = ((), (), s32[]{:S(2)}) async-start(), calls=%async_computation.3 | async-start | bytes 17301504 | tf_op jit(solution)/shard_map/all_gather | solution.py:10
  12.3 10.1 %copy-start.3 = (bf16[512,512]{0,1:T(8,128)(2,1)}, bf16[512,512]{0,1:T(8,128)(2,1)S(1)}, u32[]{:S(2)}) copy-start(bf16[512,512]{0,1:T(8,128)(2,1)S(1)} %copy.154) | copy-start | bytes 1572868
  22.5 1.0 copy-start.5
  111.4 3.4 %slice-start = ((f32[32,8,128,128]{3,2,1,0:T(8,128)}), f32[32,4,128,128]{3,2,1,0:T(8,128)S(1)}, s32[]{:S(2)}) async-start(f32[32,8,128,128]{3,2,1,0:T(8,128)} %all-gather.2.cloned.1.call-done), calls=%async_computation.4 | async-start | bytes 16777216 | tf_op jit(solution)/shard_map/split | solution.py:11
  114.8 8.8 %copy-start.1 = (f32[512,4,128]{2,0,1:T(8,128)S(1)}, f32[512,4,128]{2,0,1:T(8,128)}, u32[]{:S(2)}) copy-start(f32[512,4,128]{2,0,1:T(8,128)} %convolution_bitcast_fusion.1) | copy-start | bytes 3145732
  127.2 41.6 %all-to-all-start = ((bf16[16,32,512]{2,1,0:T(8,128)(2,1)}), bf16[16,32,512]{2,1,0:T(8,128)(2,1)}, u32[]{:S(2)}, u32[]{:S(2)}) async-start(bf16[16,32,512]{2,1,0:T(8,128)(2,1)} %all_to_all.42), calls=%async_computation | async-start | bytes 1048576 | tf_op jit(solution)/shard_map/all_to_all | solution.py:116
  142.5 4.3 %copy-start.2 = (f32[512,4,128]{2,0,1:T(8,128)S(1)}, f32[512,4,128]{2,0,1:T(8,128)}, u32[]{:S(2)}) copy-start(f32[512,4,128]{2,0,1:T(8,128)} %convolution_bitcast_fusion) | copy-start | bytes 3145732
  146.6 28.8 %copy-start.4 = (bf16[512,512]{0,1:T(8,128)(2,1)S(1)}, bf16[512,512]{0,1:T(8,128)(2,1)}, u32[]{:S(2)}) copy-start(bf16[512,512]{0,1:T(8,128)(2,1)} %copy-done.3) | copy-start | bytes 1572868
  168.8 35.7 %all-to-all-start.1 = ((bf16[16,32,512]{2,1,0:T(8,128)(2,1)}), bf16[16,32,512]{2,1,0:T(8,128)(2,1)S(1)}, u32[]{:S(2)}, u32[]{:S(2)}) async-start(bf16[16,32,512]{2,1,0:T(8,128)(2,1)} %all_to_all.46), calls=%async_computation.1 | async-start | bytes 1048576 | tf_op jit(solution)/shard_map/all_to_all | solution.py:117
  204.5 35.6 %all-to-all-start.2 = ((bf16[16,32,512]{2,1,0:T(8,128)(2,1)}), bf16[16,32,512]{2,1,0:T(8,128)(2,1)S(1)}, u32[]{:S(2)}, u32[]{:S(2)}) async-start(bf16[16,32,512]{2,1,0:T(8,128)(2,1)} %all_to_all.50), calls=%async_computation.2 | async-start | bytes 1048576 | tf_op jit(solution)/shard_map/all_to_all | solution.py:118
Sparse Core Ops, SparseCore 0:
  19.1 92.2 all-gather.1
where the time goes:
time: 249 us; the launch traced here: 248 us
  waiting for transfers between devices  154 us (62%)
  starting transfers between devices  25.4 us (10%)
  matrix products  22.7 us (9%)
  local copies, waits for them, and re-layouts  18 us (7%)
  between operations  14.3 us (6%)
  other arithmetic  13.6 us (5%)
    all_gather x1, waiting for transfers between devices, sent_together(): filled = lax.all_gather(both, axis, axis=dim, tiled=True)  83.9 us
    all_to_all x1, waiting for transfers between devices, body(): lax.all_to_all(grad_v, 'head', split_axis=0, concat_axis=1, tiled=True)  26.4 us
    all_to_all x1, waiting for transfers between devices, body(): lax.all_to_all(grad_k, 'head', split_axis=0, concat_axis=1, tiled=True)  24.2 us
    all_to_all x1, waiting for transfers between devices, body(): lax.all_to_all(grad_q, 'head', split_axis=0, concat_axis=1, tiled=True)  19.2 us
    all_to_all x1, starting transfers between devices, body(): lax.all_to_all(grad_q, 'head', split_axis=0, concat_axis=1, tiled=True)  12.3 us
    dot_general x1, matrix products, body(): jnp.einsum('ih,ihde->hde', mixing_fwd, gathered_fwd, precision=lax.Precis...  8.77 us
    all_to_all x1, starting transfers between devices, body(): lax.all_to_all(grad_k, 'head', split_axis=0, concat_axis=1, tiled=True)  6.56 us
    all_to_all x1, starting transfers between devices, body(): lax.all_to_all(grad_v, 'head', split_axis=0, concat_axis=1, tiled=True)  6.42 us
  transfers between devices with their start and end apart: 4, of which 4 were waited for; matrix products, arithmetic and copies ran while one was open for 9% of the time, Pallas kernels for 0%

commit v1 on v0

v1 whole, which is shorter than its diff:
```python
import functools

import jax
import jax.numpy as jnp
from jax import lax
from jax.experimental import pallas as pl
from jax.experimental.pallas import tpu as pltpu
from jax.sharding import PartitionSpec as P

BF16 = jnp.bfloat16
F32 = jnp.float32
FAR = 1 << 30


def doc_starts(docs_ref, docs):
    starts = [jnp.int32(0)]
    for i in range(docs - 1):
        starts.append(starts[-1] + docs_ref[i])
    return starts


def last_start(starts, position):
    found = jnp.int32(-1)
    for s in starts:
        found = jnp.maximum(found, jnp.where(s <= position, s, -1))
    return found


def next_start(starts, position):
    found = jnp.int32(FAR)
    for s in starts:
        found = jnp.minimum(found, jnp.where(s > position, s, FAR))
    return found


def dot(a, b, da, db):
    return lax.dot_general(a, b, (((da,), (db,)), ((), ())), preferred_element_type=F32)


def fetch(refs, buffer, sems, hd, head):
    return [
        pltpu.make_async_copy(
            ref.at[:, pl.ds(head * hd, hd)], buffer.at[i, head], sems.at[i, head]
        )
        for i, ref in enumerate(refs)
    ]


def summary_kernel(
    length, docs, heads, rates_ref, docs_ref, k_ref, v_ref, q_ref, g_ref, out_ref, held, sems
):
    hd = out_ref.shape[-1]
    copies = [fetch((k_ref, v_ref, q_ref, g_ref), held, sems, hd, h) for h in range(heads)]
    for group in copies:
        for copy in group:
            copy.start()
    first = lax.axis_index("seq") * length
    starts = doc_starts(docs_ref, docs)
    from_here = last_start(starts, first + length - 1) - first
    until_here = next_start(starts, first) - first
    token = lax.broadcasted_iota(jnp.int32, (1, length), 1)
    offset = token.astype(F32)
    for h in range(heads):
        rate = rates_ref[h]
        weight_k = jnp.where(token >= from_here, jnp.exp(-rate * (length - 1.0 - offset)), 0.0)
        weight_q = jnp.where(token < until_here, jnp.exp(-rate * offset), 0.0)
        for way, weight in enumerate((weight_k, weight_q)):
            copies[h][2 * way].wait()
            weighted = (held[2 * way, h].T.astype(F32) * weight).astype(BF16)
            copies[h][2 * way + 1].wait()
            out_ref[way, h] = dot(weighted, held[2 * way + 1, h], 1, 0)


def local_kernel(
    length, docs, heads, blocks,
    rates_ref, docs_ref, q_ref, k_ref, v_ref, g_ref,
    lq_ref, lk_ref, lv_ref, keep_ref,
):
    head = pl.program_id(0)
    rate = rates_ref[head]
    first = lax.axis_index("seq") * length
    starts = doc_starts(docs_ref, docs)
    t = lax.broadcasted_iota(jnp.int32, (length, length), 0)
    u = lax.broadcasted_iota(jnp.int32, (length, length), 1)
    column = lax.broadcasted_iota(jnp.int32, (length, 1), 0)
    own = jnp.full((length, 1), -FAR, jnp.int32)
    for s in starts:
        here = s - first
        own = jnp.maximum(own, jnp.where(column >= here, here, -FAR))
    distance = (t - u).astype(F32)
    allowed = (u >= own) & (u <= t)
    decayed = jnp.where(allowed, jnp.exp(-rate * jnp.maximum(distance, 0.0)), 0.0)
    q, k, v, g = q_ref[...], k_ref[...], v_ref[...], g_ref[...]
    weights_p = (decayed * dot(g, v, 1, 1)).astype(BF16)
    lq_ref[...] = dot(weights_p, k, 1, 0)
    lk_ref[...] = dot(weights_p, q, 0, 0)
    weights_a = (decayed * dot(q, k, 1, 1)).astype(BF16)
    lv_ref[...] = dot(weights_a, g, 0, 0)

    @pl.when(head == 0)
    def _():
        me = lax.axis_index("seq")
        per_way = blocks // 2
        backward = me // per_way
        mine = rates_ref[(me % per_way) // (per_way // heads)]
        low = lax.broadcasted_iota(jnp.int32, keep_ref.shape, 0) * length + backward
        broken = low < 0
        for s in starts:
            broken = broken | ((s >= low) & (s < low + length))
        decay = jnp.exp(jnp.full(keep_ref.shape, -mine * length, F32))
        keep_ref[...] = jnp.where(broken, 0.0, decay)


def scan_kernel(blocks, keep_ref, in_ref, out_ref):
    backward = lax.axis_index("seq") // (blocks // 2)
    carry = jnp.zeros(in_ref.shape[1:], F32)
    for i in range(blocks):
        j = jnp.where(backward == 1, blocks - 1 - i, i)
        out_ref[j] = carry.astype(BF16)
        carry = keep_ref[pl.ds(j, 1), :] * carry + in_ref[j]


def final_kernel(
    length, docs, heads,
    rates_ref, docs_ref, g_ref, v_ref, k_ref, lq_ref, lk_ref, lv_ref, s_ref,
    out_ref, held, local, ready, sems, local_sems, out_sems,
):
    _, parts, _, rows, _ = ready.shape
    hd = s_ref.shape[-1]
    copies = [
        fetch((g_ref, v_ref, k_ref), held, sems, hd, h)
        + fetch((lq_ref, lk_ref, lv_ref), local, local_sems, hd, h)
        for h in range(heads)
    ]
    for group in copies:
        for copy in group:
            copy.start()
    first = lax.axis_index("seq") * length
    starts = doc_starts(docs_ref, docs)
    until_here = next_start(starts, first - 1) - first
    from_here = last_start(starts, first + length) - first
    row = lax.broadcasted_iota(jnp.int32, (length, hd), 0)
    offset = row.astype(F32)
    written = []
    for h in range(heads):
        rate = rates_ref[h]
        factor_in = jnp.where(row < until_here, jnp.exp(-rate * (offset + 1.0)), 0.0)
        factor_back = jnp.where(row >= from_here, jnp.exp(-rate * (length - offset)), 0.0)
        matrices = (s_ref[0, h], s_ref[1, h], s_ref[1, h])
        factors = (factor_in, factor_back, factor_back)
        for copy in copies[h]:
            copy.wait()
        for i in range(3):
            outer = dot(held[i, h], matrices[i], 1, 0 if i == 2 else 1) * factors[i]
            grad = (local[i, h] + outer).astype(BF16)
            ready[h, :, i] = grad.reshape(parts, rows, hd)
        written.append(
            pltpu.make_async_copy(
                ready.at[h], out_ref.at[:, :, :, pl.ds(h * hd, hd)], out_sems.at[h]
            )
        )
        written[h].start()
    for copy in written:
        copy.wait()


def spread_kernel(in_ref, *refs):
    outs, sems = refs[:3], refs[3]
    parts, _, _, width = in_ref.shape
    copies = []
    for i in range(3):
        for h in range(parts):
            copy = pltpu.make_async_copy(
                in_ref.at[h, i], outs[i].at[:, pl.ds(h * width, width)], sems.at[i, h]
            )
            copy.start()
            copies.append(copy)
    for copy in copies:
        copy.wait()


def on_chip(array):
    return pltpu.with_memory_space_constraint(array, pltpu.VMEM)


def body(queries, keys, values, grad_out, rates, doc_lengths):
    length, inner = queries.shape
    heads = rates.shape[0]
    docs = doc_lengths.shape[0]
    hd = inner // heads
    blocks = lax.axis_size("seq")
    parts = lax.axis_size("head")
    rows = length // parts
    smem = pl.BlockSpec(memory_space=pltpu.SMEM)
    per_head = pl.BlockSpec((length, hd), lambda h: (0, h))
    anywhere = pl.BlockSpec(memory_space=pl.ANY)
    vmem = pl.BlockSpec(memory_space=pltpu.VMEM)
    summary = pl.pallas_call(
        functools.partial(summary_kernel, length, docs, heads),
        in_specs=[smem, smem] + [anywhere] * 4,
        out_specs=vmem,
        out_shape=jax.ShapeDtypeStruct((2, heads, hd, hd), F32),
        scratch_shapes=[
            pltpu.VMEM((4, heads, length, hd), BF16),
            pltpu.SemaphoreType.DMA((4, heads)),
        ],
        name="summary",
    )(rates, doc_lengths, keys, values, queries, grad_out)
    piece = 2 * heads * hd // blocks
    swapped = lax.all_to_all(
        summary.reshape(blocks, piece, hd), "seq", split_axis=0, concat_axis=0, tiled=True
    )
    *local, keep = pl.pallas_call(
        functools.partial(local_kernel, length, docs, heads, blocks),
        grid=(heads,),
        in_specs=[smem, smem] + [per_head] * 4,
        out_specs=[per_head] * 3
        + [pl.BlockSpec((blocks, hd), lambda h: (0, 0))],
        out_shape=[jax.ShapeDtypeStruct((length, inner), F32)] * 3
        + [jax.ShapeDtypeStruct((blocks, hd), F32)],
        name="local",
    )(rates, doc_lengths, queries, keys, values, grad_out)
    scanned = pl.pallas_call(
        functools.partial(scan_kernel, blocks),
        in_specs=[vmem, vmem],
        out_specs=vmem,
        out_shape=jax.ShapeDtypeStruct((blocks, piece, hd), BF16),
        compiler_params=pltpu.CompilerParams(vmem_limit_bytes=4 << 20),
        name="scan",
    )(keep, on_chip(swapped))
    returned = lax.all_to_all(scanned, "seq", split_axis=0, concat_axis=0, tiled=True)
    grads = pl.pallas_call(
        functools.partial(final_kernel, length, docs, heads),
        in_specs=[smem, smem] + [anywhere] * 6 + [vmem],
        out_specs=anywhere,
        out_shape=jax.ShapeDtypeStruct((parts, 3, rows, inner), BF16),
        scratch_shapes=[
            pltpu.VMEM((3, heads, length, hd), BF16),
            pltpu.VMEM((3, heads, length, hd), F32),
            pltpu.VMEM((heads, parts, 3, rows, hd), BF16),
            pltpu.SemaphoreType.DMA((3, heads)),
            pltpu.SemaphoreType.DMA((3, heads)),
            pltpu.SemaphoreType.DMA((heads,)),
        ],
        name="final",
    )(
        rates, doc_lengths, grad_out, values, keys, *local,
        on_chip(returned.reshape(2, heads, hd, hd)),
    )
    moved = lax.all_to_all(
        grads.reshape(parts, 3 * rows, inner), "head", split_axis=0, concat_axis=0, tiled=True
    ).reshape(parts, 3, rows, inner)
    return pl.pallas_call(
        spread_kernel,
        in_specs=[pl.BlockSpec(memory_space=pl.ANY)],
        out_specs=[pl.BlockSpec(memory_space=pl.ANY)] * 3,
        out_shape=[jax.ShapeDtypeStruct((rows, parts * inner), BF16)] * 3,
        scratch_shapes=[pltpu.SemaphoreType.DMA((3, parts))],
        compiler_params=pltpu.CompilerParams(vmem_limit_bytes=4 << 20),
        name="spread",
    )(moved)


def solution(mesh):
    return jax.shard_map(
        body,
        mesh=mesh,
        in_specs=(
            P("seq", "head"),
            P("seq", "head"),
            P("seq", "head"),
            P("seq", "head"),
            P("head"),
            P(),
        ),
        out_specs=(P(("seq", "head"), None), P(("seq", "head"), None), P(("seq", "head"), None)),
        check_vma=False,
    )
```

time: 249 us -> 134 us (0.54)
  the two profiles are of different devices: /device:TPU:2 before, /device:TPU:32 now
where the time goes in v1:
time: 134 us; the launch traced here: 133 us
  blocking collectives  102 us (76%)
  Pallas kernels  18.6 us (14%)
  starting transfers between devices  7.33 us (5%)
  waiting for transfers between devices  3.67 us (3%)
    all_to_all x1, blocking collectives, body(): lax.all_to_all(grads.reshape(parts, 3 * rows, inner), 'head', split_axis=...  90 us
    all_to_all x1, blocking collectives, body(): lax.all_to_all(scanned, 'seq', split_axis=0, concat_axis=0, tiled=True)  12.3 us
    pallas_call x1, Pallas kernels, body(): pl.pallas_call(functools.partial(local_kernel, length, docs, heads, block...  7.92 us
    all_to_all x1, starting transfers between devices, body(): lax.all_to_all(summary.reshape(blocks, piece, hd), 'seq', split_axis=0, c...  7.33 us
    pallas_call x1, Pallas kernels, body(): pl.pallas_call(functools.partial(summary_kernel, length, docs, heads), in...  4.65 us
    pallas_call x1, Pallas kernels, body(): pl.pallas_call(functools.partial(final_kernel, length, docs, heads), in_s...  4.43 us
    all_to_all x1, waiting for transfers between devices, body(): lax.all_to_all(summary.reshape(blocks, piece, hd), 'seq', split_axis=0, c...  3.67 us
  transfers between devices with their start and end apart: 1, of which 1 were waited for; matrix products, arithmetic and copies ran while one was open for 0% of the time, Pallas kernels for 6%

profile of v1, /device:TPU:32, one launch (start us, length us, event | category | flops | bytes accessed | tf_op | source)
XLA Modules:
  0.0 133.3 jit_solution(8160995485676750375)
XLA Ops:
  0.6 4.7 %summary.1 = f32[2,4,128,128]{3,2,1,0:T(8,128)} custom-call(f32[4]{0:T(128)} %rates_ref.5, s32[8]{0:T(128)} %docs_ref.5, bf16[512,512]{1,0:T(8,128)(2,1)} %k_ref.5, bf16[512,512]{1,0:T(8,128)(2,1)} %v_ref.5, bf16[512,512]{1,0:T(8,128)(2,1)} %q_ref.3, bf16[512,512]{1,0:T(8,128)(2,1)} %g_ref.5), custom_call_target="tpu_custom_call" | custom-call | tf_op jit(solution)/shard_map/summary/pallas_call | solution.py:198
  5.3 7.3 %all-to-all-start = ((f32[32,32,128]{2,1,0:T(8,128)}), f32[32,32,128]{2,1,0:T(8,128)S(1)}, u32[]{:S(2)}, u32[]{:S(2)}) async-start(f32[32,32,128]{2,1,0:T(8,128)} %bitcast.7), calls=%async_computation | async-start | bytes 1048576 | tf_op jit(solution)/shard_map/all_to_all | solution.py:210
  12.6 7.9 %local.1 = (f32[512,512]{1,0:T(8,128)}, f32[512,512]{1,0:T(8,128)}, f32[512,512]{1,0:T(8,128)}, f32[32,128]{1,0:T(8,128)}) custom-call(f32[4]{0:T(128)} %rates_ref.5, s32[8]{0:T(128)} %docs_ref.5, bf16[512,512]{1,0:T(8,128)(2,1)} %q_ref.3, bf16[512,512]{1,0:T(8,128)(2,1)} %k_ref.5, bf16[512,512]{1,0:T(8,128)(2,1)} %v_ref.5, bf16[512,512]{1,0:T(8,128)(2,1)} %g_ref.5), custom_call_target="tpu_custom_call" | custom-call | tf_op jit(solution)/shard_map/local/pallas_call | solution.py:213
  20.6 3.7 %all-to-all-done.in_ref = f32[32,32,128]{2,1,0:T(8,128)S(1)} async-done(((f32[32,32,128]{2,1,0:T(8,128)}), f32[32,32,128]{2,1,0:T(8,128)S(1)}, u32[]{:S(2)}, u32[]{:S(2)}) %all-to-all-start) | async-done | bytes 524320 | tf_op jit(solution)/shard_map/all_to_all | solution.py:210
  24.2 0.0 copy-start
  24.2 0.7 copy-done
  24.9 0.1 scan.1
  25.0 12.3 %all_to_all.15 = bf16[32,32,128]{2,1,0:T(8,128)(2,1)S(1)} all-to-all(bf16[32,32,128]{2,1,0:T(8,128)(2,1)S(1)} %scan.1), channel_id=1, replica_groups=mesh['seq'=32,'head'=16] {'seq'}, dimensions={0} | all-to-all | bytes 524288 | tf_op jit(solution)/shard_map/all_to_all | solution.py:231
  37.3 4.4 %final.1 = bf16[16,3,32,512]{3,2,1,0:T(8,128)(2,1)} custom-call(f32[4]{0:T(128)} %rates_ref.5, s32[8]{0:T(128)} %docs_ref.5, bf16[512,512]{1,0:T(8,128)(2,1)} %g_ref.5, bf16[512,512]{1,0:T(8,128)(2,1)} %v_ref.5, bf16[512,512]{1,0:T(8,128)(2,1)} %k_ref.5, f32[512,512]{1,0:T(8,128)} %get-tuple-element.7.lq_ref, f32[512,512]{1,0:T(8,128)} %get-tuple-element.8.lk_ref, ...), custom_call_target="tpu_custom_call" | custom-call | tf_op jit(solution)/shard_map/final/pallas_call | solution.py:232
  41.8 90.0 %all_to_all.16 = bf16[16,96,512]{2,1,0:T(8,128)(2,1)S(1)} all-to-all(bf16[16,96,512]{2,1,0:T(8,128)(2,1)} %bitcast.6), channel_id=1, replica_groups=mesh['seq'=32,'head'=16] {'head'}, dimensions={0} | all-to-all | bytes 3145728 | tf_op jit(solution)/shard_map/all_to_all | solution.py:250
  131.7 1.5 %spread.1 = (bf16[32,8192]{1,0:T(8,128)(2,1)}, bf16[32,8192]{1,0:T(8,128)(2,1)}, bf16[32,8192]{1,0:T(8,128)(2,1)}) custom-call(bf16[16,3,32,512]{3,2,1,0:T(8,128)(2,1)S(1)} %bitcast.4), custom_call_target="tpu_custom_call" | custom-call | tf_op jit(solution)/shard_map/spread/pallas_call | solution.py:253
Async XLA Ops:
  5.3 18.9 %all-to-all-start = ((f32[32,32,128]{2,1,0:T(8,128)}), f32[32,32,128]{2,1,0:T(8,128)S(1)}, u32[]{:S(2)}, u32[]{:S(2)}) async-start(f32[32,32,128]{2,1,0:T(8,128)} %bitcast.7), calls=%async_computation | async-start | bytes 1048576 | tf_op jit(solution)/shard_map/all_to_all | solution.py:210
  24.2 0.7 copy-start

commit v2 on v1

--- a/solution.py
+++ b/solution.py
@@ -37,40 +37,51 @@
     return lax.dot_general(a, b, (((da,), (db,)), ((), ())), preferred_element_type=F32)
 
 
-def fetch(refs, buffer, sems, hd, head):
+def start_all(copies):
+    for copy in copies:
+        copy.start()
+
+
+def fetch(refs, buffers, sems):
     return [
-        pltpu.make_async_copy(
-            ref.at[:, pl.ds(head * hd, hd)], buffer.at[i, head], sems.at[i, head]
-        )
-        for i, ref in enumerate(refs)
+        pltpu.make_async_copy(ref, buffer, sems.at[i])
+        for i, (ref, buffer) in enumerate(zip(refs, buffers))
     ]
 
 
 def summary_kernel(
-    length, docs, heads, rates_ref, docs_ref, k_ref, v_ref, q_ref, g_ref, out_ref, held, sems
+    length, docs, heads,
+    rates_hbm, docs_hbm, k_hbm, v_hbm, q_hbm, g_hbm, sums,
+    rates_ref, docs_ref, held, sems,
 ):
-    hd = out_ref.shape[-1]
-    copies = [fetch((k_ref, v_ref, q_ref, g_ref), held, sems, hd, h) for h in range(heads)]
-    for group in copies:
-        for copy in group:
-            copy.start()
+    hd = sums.shape[-1]
+    copies = fetch(
+        (docs_hbm, rates_hbm, k_hbm, v_hbm, q_hbm, g_hbm),
+        (docs_ref, rates_ref, *(held.at[i] for i in range(4))),
+        sems,
+    )
+    start_all(copies)
+    copies[0].wait()
     first = lax.axis_index("seq") * length
     starts = doc_starts(docs_ref, docs)
     from_here = last_start(starts, first + length - 1) - first
     until_here = next_start(starts, first) - first
     token = lax.broadcasted_iota(jnp.int32, (1, length), 1)
     offset = token.astype(F32)
-    for h in range(heads):
-        rate = rates_ref[h]
-        weight_k = jnp.where(token >= from_here, jnp.exp(-rate * (length - 1.0 - offset)), 0.0)
-        weight_q = jnp.where(token < until_here, jnp.exp(-rate * offset), 0.0)
-        for way, weight in enumerate((weight_k, weight_q)):
-            copies[h][2 * way].wait()
-            weighted = (held[2 * way, h].T.astype(F32) * weight).astype(BF16)
-            copies[h][2 * way + 1].wait()
-            out_ref[way, h] = dot(weighted, held[2 * way + 1, h], 1, 0)
-
-
+    copies[1].wait()
+    for way in range(2):
+        copies[2 + 2 * way].wait()
+        copies[3 + 2 * way].wait()
+        for h in range(heads):
+            at = slice(h * hd, (h + 1) * hd)
+            rate = rates_ref[h]
+            if way == 0:
+                decayed = jnp.exp(-rate * (length - 1.0 - offset))
+                weight = jnp.where(token >= from_here, decayed, 0.0)
+            else:
+                weight = jnp.where(token < until_here, jnp.exp(-rate * offset), 0.0)
+            weighted = (held[2 * way, :, at].T.astype(F32) * weight).astype(BF16)
+            sums[way, h] = dot(weighted, held[2 * way + 1, :, at], 1, 0)
 def local_kernel(
     length, docs, heads, blocks,
     rates_ref, docs_ref, q_ref, k_ref, v_ref, g_ref,
@@ -122,46 +133,50 @@
 
 def final_kernel(
     length, docs, heads,
-    rates_ref, docs_ref, g_ref, v_ref, k_ref, lq_ref, lk_ref, lv_ref, s_ref,
-    out_ref, held, local, ready, sems, local_sems, out_sems,
+    rates_hbm, docs_hbm, g_hbm, v_hbm, k_hbm, lq_hbm, lk_hbm, lv_hbm, s_ref, out_ref,
+    rates_ref, docs_ref, held, local, factors, sems,
 ):
-    _, parts, _, rows, _ = ready.shape
+    parts, _, rows, _ = out_ref.shape
     hd = s_ref.shape[-1]
-    copies = [
-        fetch((g_ref, v_ref, k_ref), held, sems, hd, h)
-        + fetch((lq_ref, lk_ref, lv_ref), local, local_sems, hd, h)
-        for h in range(heads)
-    ]
-    for group in copies:
-        for copy in group:
-            copy.start()
+    copies = fetch(
+        (docs_hbm, rates_hbm, g_hbm, lq_hbm, v_hbm, lk_hbm, k_hbm, lv_hbm),
+        (docs_ref, rates_ref) + sum(((held.at[i], local.at[i]) for i in range(3)), ()),
+        sems,
+    )
+    start_all(copies)
+    copies[0].wait()
     first = lax.axis_index("seq") * length
     starts = doc_starts(docs_ref, docs)
     until_here = next_start(starts, first - 1) - first
     from_here = last_start(starts, first + length) - first
-    row = lax.broadcasted_iota(jnp.int32, (length, hd), 0)
-    offset = row.astype(F32)
-    written = []
+    group = 64
+    row = lax.broadcasted_iota(jnp.int32, (group, hd), 0)
+    near = row.astype(F32)
+    copies[1].wait()
     for h in range(heads):
         rate = rates_ref[h]
-        factor_in = jnp.where(row < until_here, jnp.exp(-rate * (offset + 1.0)), 0.0)
-        factor_back = jnp.where(row >= from_here, jnp.exp(-rate * (length - offset)), 0.0)
-        matrices = (s_ref[0, h], s_ref[1, h], s_ref[1, h])
-        factors = (factor_in, factor_back, factor_back)
-        for copy in copies[h]:
-            copy.wait()
-        for i in range(3):
-            outer = dot(held[i, h], matrices[i], 1, 0 if i == 2 else 1) * factors[i]
-            grad = (local[i, h] + outer).astype(BF16)
-            ready[h, :, i] = grad.reshape(parts, rows, hd)
-        written.append(
-            pltpu.make_async_copy(
-                ready.at[h], out_ref.at[:, :, :, pl.ds(h * hd, hd)], out_sems.at[h]
-            )
-        )
-        written[h].start()
-    for copy in written:
-        copy.wait()
+        ahead = jnp.exp(-rate * (near + 1.0))
+        behind = jnp.exp(-rate * (group - near))
+        for low in range(0, length, group):
+            these = slice(low, low + group)
+            far = jnp.exp(jnp.full((1, hd), -rate * low, F32))
+            factors[0, h, these] = jnp.where(row < until_here - low, ahead * far, 0.0)
+            far = jnp.exp(jnp.full((1, hd), -rate * (length - group - low), F32))
+            factors[1, h, these] = jnp.where(row >= from_here - low, behind * far, 0.0)
+
+    size = length // 1
+    for i in range(3):
+        copies[2 + 2 * i].wait()
+        copies[3 + 2 * i].wait()
+        for h in range(heads):
+            at = slice(h * hd, (h + 1) * hd)
+            matrix = s_ref[min(i, 1), h]
+            for low in range(0, length, size):
+                these = slice(low, low + size)
+                outer = dot(held[i, these, at], matrix, 1, 0 if i == 2 else 1)
+                grad = local[i, these, at] + outer * factors[min(i, 1), h, these]
+                into = slice(low // rows, (low + size) // rows)
+                out_ref[into, i, :, at] = grad.astype(BF16).reshape(size // rows, rows, hd)
 
 
 def spread_kernel(in_ref, *refs):
@@ -197,12 +212,14 @@
     vmem = pl.BlockSpec(memory_space=pltpu.VMEM)
     summary = pl.pallas_call(
         functools.partial(summary_kernel, length, docs, heads),
-        in_specs=[smem, smem] + [anywhere] * 4,
+        in_specs=[anywhere] * 6,
         out_specs=vmem,
-        out_shape=jax.ShapeDtypeStruct((2, heads, hd, hd), F32),
+        out_shape=pltpu.VMEM((2, heads, hd, hd), F32),
         scratch_shapes=[
-            pltpu.VMEM((4, heads, length, hd), BF16),
-            pltpu.SemaphoreType.DMA((4, heads)),
+            pltpu.SMEM((heads,), F32),
+            pltpu.SMEM((docs,), jnp.int32),
+            pltpu.VMEM((4, length, inner), BF16),
+            pltpu.SemaphoreType.DMA((6,)),
         ],
         name="summary",
     )(rates, doc_lengths, keys, values, queries, grad_out)
@@ -217,7 +234,7 @@
         out_specs=[per_head] * 3
         + [pl.BlockSpec((blocks, hd), lambda h: (0, 0))],
         out_shape=[jax.ShapeDtypeStruct((length, inner), F32)] * 3
-        + [jax.ShapeDtypeStruct((blocks, hd), F32)],
+        + [pltpu.VMEM((blocks, hd), F32)],
         name="local",
     )(rates, doc_lengths, queries, keys, values, grad_out)
     scanned = pl.pallas_call(
@@ -227,20 +244,20 @@
         out_shape=jax.ShapeDtypeStruct((blocks, piece, hd), BF16),
         compiler_params=pltpu.CompilerParams(vmem_limit_bytes=4 << 20),
         name="scan",
-    )(keep, on_chip(swapped))
+    )(on_chip(keep), on_chip(swapped))
     returned = lax.all_to_all(scanned, "seq", split_axis=0, concat_axis=0, tiled=True)
     grads = pl.pallas_call(
         functools.partial(final_kernel, length, docs, heads),
-        in_specs=[smem, smem] + [anywhere] * 6 + [vmem],
-        out_specs=anywhere,
-        out_shape=jax.ShapeDtypeStruct((parts, 3, rows, inner), BF16),
+        in_specs=[anywhere] * 8 + [vmem],
+        out_specs=vmem,
+        out_shape=pltpu.VMEM((parts, 3, rows, inner), BF16),
         scratch_shapes=[
-            pltpu.VMEM((3, heads, length, hd), BF16),
-            pltpu.VMEM((3, heads, length, hd), F32),
-            pltpu.VMEM((heads, parts, 3, rows, hd), BF16),
-            pltpu.SemaphoreType.DMA((3, heads)),
-            pltpu.SemaphoreType.DMA((3, heads)),
-            pltpu.SemaphoreType.DMA((heads,)),
+            pltpu.SMEM((heads,), F32),
+            pltpu.SMEM((docs,), jnp.int32),
+            pltpu.VMEM((3, length, inner), BF16),
+            pltpu.VMEM((3, length, inner), F32),
+            pltpu.VMEM((2, heads, length, hd), F32),
+            pltpu.SemaphoreType.DMA((8,)),
         ],
         name="final",
     )(

time: 134 us -> 129 us (0.963)
  Pallas kernels: 18.6 us -> 15 us
    pallas_call x1, Pallas kernels: 4.65 us -> 2.76 us  [body(): pl.pallas_call(functools.partial(summary_kernel, length, docs, heads), in...]
    pallas_call x1, Pallas kernels: 4.43 us -> 2.69 us  [body(): pl.pallas_call(functools.partial(final_kernel, length, docs, heads), in_s...]
where the time goes in v2:
time: 129 us
  blocking collectives  102 us (79%)
  Pallas kernels  15 us (12%)
  starting transfers between devices  7.33 us (6%)
  waiting for transfers between devices  3.65 us (3%)
    all_to_all x1, blocking collectives, body(): lax.all_to_all(grads.reshape(parts, 3 * rows, inner), 'head', split_axis=...  89.8 us
    all_to_all x1, blocking collectives, body(): lax.all_to_all(scanned, 'seq', split_axis=0, concat_axis=0, tiled=True)  12.3 us
    pallas_call x1, Pallas kernels, body(): pl.pallas_call(functools.partial(local_kernel, length, docs, heads, block...  7.95 us
    all_to_all x1, starting transfers between devices, body(): lax.all_to_all(summary.reshape(blocks, piece, hd), 'seq', split_axis=0, c...  7.33 us
    all_to_all x1, waiting for transfers between devices, body(): lax.all_to_all(summary.reshape(blocks, piece, hd), 'seq', split_axis=0, c...  3.65 us
    pallas_call x1, Pallas kernels, body(): pl.pallas_call(functools.partial(summary_kernel, length, docs, heads), in...  2.76 us
    pallas_call x1, Pallas kernels, body(): pl.pallas_call(functools.partial(final_kernel, length, docs, heads), in_s...  2.69 us
  transfers between devices with their start and end apart: 1, of which 1 were waited for; matrix products, arithmetic and copies ran while one was open for 0% of the time, Pallas kernels for 6%

profile of v2, /device:TPU:32, one launch (start us, length us, event | category | flops | bytes accessed | tf_op | source)
XLA Modules:
  0.0 128.8 jit_solution(9314076774984869579)
XLA Ops:
  0.6 2.8 %summary.1 = f32[2,4,128,128]{3,2,1,0:T(8,128)} custom-call(f32[4]{0:T(128)} %rates_hbm.3, s32[8]{0:T(128)} %docs_hbm.3, bf16[512,512]{1,0:T(8,128)(2,1)} %k_hbm.3, bf16[512,512]{1,0:T(8,128)(2,1)} %v_hbm.3, bf16[512,512]{1,0:T(8,128)(2,1)} %q_hbm.1, bf16[512,512]{1,0:T(8,128)(2,1)} %g_hbm.3), custom_call_target="tpu_custom_call" | custom-call | tf_op jit(solution)/shard_map/summary/pallas_call | solution.py:213
  3.4 7.3 %all-to-all-start = ((f32[32,32,128]{2,1,0:T(8,128)}), f32[32,32,128]{2,1,0:T(8,128)S(1)}, u32[]{:S(2)}, u32[]{:S(2)}) async-start(f32[32,32,128]{2,1,0:T(8,128)} %bitcast), calls=%async_computation | async-start | bytes 1048576 | tf_op jit(solution)/shard_map/all_to_all | solution.py:227
  10.7 7.9 %local.1 = (f32[512,512]{1,0:T(8,128)}, f32[512,512]{1,0:T(8,128)}, f32[512,512]{1,0:T(8,128)}, f32[32,128]{1,0:T(8,128)S(1)}) custom-call(f32[4]{0:T(128)} %rates_hbm.3, s32[8]{0:T(128)} %docs_hbm.3, bf16[512,512]{1,0:T(8,128)(2,1)} %q_hbm.1, bf16[512,512]{1,0:T(8,128)(2,1)} %k_hbm.3, bf16[512,512]{1,0:T(8,128)(2,1)} %v_hbm.3, bf16[512,512]{1,0:T(8,128)(2,1)} %g_hbm.3), custom_call_target="tpu_custom_call" | custom-call | tf_op jit(solution)/shard_map/local/pallas_call | solution.py:230
  18.7 3.6 %all-to-all-done.in_ref = f32[32,32,128]{2,1,0:T(8,128)S(1)} async-done(((f32[32,32,128]{2,1,0:T(8,128)}), f32[32,32,128]{2,1,0:T(8,128)S(1)}, u32[]{:S(2)}, u32[]{:S(2)}) %all-to-all-start) | async-done | bytes 524320 | tf_op jit(solution)/shard_map/all_to_all | solution.py:227
  22.3 0.1 scan.1
  22.4 12.3 %all_to_all.15 = bf16[32,32,128]{2,1,0:T(8,128)(2,1)S(1)} all-to-all(bf16[32,32,128]{2,1,0:T(8,128)(2,1)S(1)} %scan.1), channel_id=1, replica_groups=mesh['seq'=32,'head'=16] {'seq'}, dimensions={0} | all-to-all | bytes 524288 | tf_op jit(solution)/shard_map/all_to_all | solution.py:248
  34.7 2.7 %final.1 = bf16[16,3,32,512]{3,2,1,0:T(8,128)(2,1)S(1)} custom-call(f32[4]{0:T(128)} %rates_hbm.3, s32[8]{0:T(128)} %docs_hbm.3, bf16[512,512]{1,0:T(8,128)(2,1)} %g_hbm.3, bf16[512,512]{1,0:T(8,128)(2,1)} %v_hbm.3, bf16[512,512]{1,0:T(8,128)(2,1)} %k_hbm.3, f32[512,512]{1,0:T(8,128)} %get-tuple-element.7.lq_hbm, f32[512,512]{1,0:T(8,128)} %get-tuple-element.8.lk_hbm, ...), custom_call_target="tpu_custom_call" | custom-call | tf_op jit(solution)/shard_map/final/pallas_call | solution.py:249
  37.4 89.8 %all_to_all.16 = bf16[16,96,512]{2,1,0:T(8,128)(2,1)S(1)} all-to-all(bf16[16,96,512]{2,1,0:T(8,128)(2,1)S(1)} %bitcast.5), channel_id=1, replica_groups=mesh['seq'=32,'head'=16] {'head'}, dimensions={0} | all-to-all | bytes 3145728 | tf_op jit(solution)/shard_map/all_to_all | solution.py:267
  127.2 1.5 %spread.1 = (bf16[32,8192]{1,0:T(8,128)(2,1)}, bf16[32,8192]{1,0:T(8,128)(2,1)}, bf16[32,8192]{1,0:T(8,128)(2,1)}) custom-call(bf16[16,3,32,512]{3,2,1,0:T(8,128)(2,1)S(1)} %bitcast.4), custom_call_target="tpu_custom_call" | custom-call | tf_op jit(solution)/shard_map/spread/pallas_call | solution.py:270
Async XLA Ops:
  3.4 18.9 %all-to-all-start = ((f32[32,32,128]{2,1,0:T(8,128)}), f32[32,32,128]{2,1,0:T(8,128)S(1)}, u32[]{:S(2)}, u32[]{:S(2)}) async-start(f32[32,32,128]{2,1,0:T(8,128)} %bitcast), calls=%async_computation | async-start | bytes 1048576 | tf_op jit(solution)/shard_map/all_to_all | solution.py:227

commit v3 on v2

--- a/solution.py
+++ b/solution.py
@@ -10,6 +10,7 @@
 BF16 = jnp.bfloat16
 F32 = jnp.float32
 FAR = 1 << 30
+LEAD = 11
 
 
 def doc_starts(docs_ref, docs):
@@ -91,22 +92,33 @@
     rate = rates_ref[head]
     first = lax.axis_index("seq") * length
     starts = doc_starts(docs_ref, docs)
-    t = lax.broadcasted_iota(jnp.int32, (length, length), 0)
-    u = lax.broadcasted_iota(jnp.int32, (length, length), 1)
-    column = lax.broadcasted_iota(jnp.int32, (length, 1), 0)
-    own = jnp.full((length, 1), -FAR, jnp.int32)
-    for s in starts:
-        here = s - first
-        own = jnp.maximum(own, jnp.where(column >= here, here, -FAR))
-    distance = (t - u).astype(F32)
-    allowed = (u >= own) & (u <= t)
-    decayed = jnp.where(allowed, jnp.exp(-rate * jnp.maximum(distance, 0.0)), 0.0)
     q, k, v, g = q_ref[...], k_ref[...], v_ref[...], g_ref[...]
-    weights_p = (decayed * dot(g, v, 1, 1)).astype(BF16)
-    lq_ref[...] = dot(weights_p, k, 1, 0)
-    lk_ref[...] = dot(weights_p, q, 0, 0)
-    weights_a = (decayed * dot(q, k, 1, 1)).astype(BF16)
-    lv_ref[...] = dot(weights_a, g, 0, 0)
+    half = length // 2
+    for low in (0, half):
+        rows, seen = slice(low, low + half), slice(0, low + half)
+        t = lax.broadcasted_iota(jnp.int32, (half, low + half), 0) + low
+        u = lax.broadcasted_iota(jnp.int32, (half, low + half), 1)
+        column = lax.broadcasted_iota(jnp.int32, (half, 1), 0) + low
+        own = jnp.full((half, 1), -FAR, jnp.int32)
+        for s in starts:
+            here = s - first
+            own = jnp.maximum(own, jnp.where(column >= here, here, -FAR))
+        distance = (t - u).astype(F32)
+        allowed = (u >= own) & (u <= t)
+        decayed = jnp.where(allowed, jnp.exp(-rate * jnp.maximum(distance, 0.0)), 0.0)
+        weights_p = (decayed * dot(g[rows], v[seen], 1, 1)).astype(BF16)
+        weights_a = (decayed * dot(q[rows], k[seen], 1, 1)).astype(BF16)
+        lq_ref[rows] = dot(weights_p, k[seen], 1, 0)
+        part_k = dot(weights_p, q[rows], 0, 0)
+        part_v = dot(weights_a, g[rows], 0, 0)
+        if low:
+            lk_ref[:half] = lk_ref[:half] + part_k[:half]
+            lk_ref[half:] = part_k[half:]
+            lv_ref[:half] = lv_ref[:half] + part_v[:half]
+            lv_ref[half:] = part_v[half:]
+        else:
+            lk_ref[:half] = part_k
+            lv_ref[:half] = part_v
 
     @pl.when(head == 0)
     def _():
@@ -132,7 +144,7 @@
 
 
 def final_kernel(
-    length, docs, heads,
+    length, docs, heads, lead,
     rates_hbm, docs_hbm, g_hbm, v_hbm, k_hbm, lq_hbm, lk_hbm, lv_hbm, s_ref, out_ref,
     rates_ref, docs_ref, held, local, factors, sems,
 ):
@@ -164,29 +176,28 @@
             far = jnp.exp(jnp.full((1, hd), -rate * (length - group - low), F32))
             factors[1, h, these] = jnp.where(row >= from_here - low, behind * far, 0.0)
 
-    size = length // 1
     for i in range(3):
         copies[2 + 2 * i].wait()
         copies[3 + 2 * i].wait()
         for h in range(heads):
             at = slice(h * hd, (h + 1) * hd)
             matrix = s_ref[min(i, 1), h]
-            for low in range(0, length, size):
-                these = slice(low, low + size)
-                outer = dot(held[i, these, at], matrix, 1, 0 if i == 2 else 1)
-                grad = local[i, these, at] + outer * factors[min(i, 1), h, these]
-                into = slice(low // rows, (low + size) // rows)
-                out_ref[into, i, :, at] = grad.astype(BF16).reshape(size // rows, rows, hd)
-
-
-def spread_kernel(in_ref, *refs):
+            outer = dot(held[i, :, at], matrix, 1, 0 if i == 2 else 1)
+            grad = (local[i, :, at] + outer * factors[min(i, 1), h]).astype(BF16)
+            grad = grad.reshape(parts, rows, hd)
+            out_ref[: parts - lead, i, :, at] = grad[lead:]
+            out_ref[parts - lead :, i, :, at] = grad[:lead]
+
+
+def spread_kernel(lead, in_ref, *refs):
     outs, sems = refs[:3], refs[3]
     parts, _, _, width = in_ref.shape
     copies = []
     for i in range(3):
         for h in range(parts):
+            column = (h + lead) % parts * width
             copy = pltpu.make_async_copy(
-                in_ref.at[h, i], outs[i].at[:, pl.ds(h * width, width)], sems.at[i, h]
+                in_ref.at[h, i], outs[i].at[:, pl.ds(column, width)], sems.at[i, h]
             )
             copy.start()
             copies.append(copy)
@@ -206,6 +217,7 @@
     blocks = lax.axis_size("seq")
     parts = lax.axis_size("head")
     rows = length // parts
+    lead = LEAD % parts
     smem = pl.BlockSpec(memory_space=pltpu.SMEM)
     per_head = pl.BlockSpec((length, hd), lambda h: (0, h))
     anywhere = pl.BlockSpec(memory_space=pl.ANY)
@@ -247,7 +259,7 @@
     )(on_chip(keep), on_chip(swapped))
     returned = lax.all_to_all(scanned, "seq", split_axis=0, concat_axis=0, tiled=True)
     grads = pl.pallas_call(
-        functools.partial(final_kernel, length, docs, heads),
+        functools.partial(final_kernel, length, docs, heads, lead),
         in_specs=[anywhere] * 8 + [vmem],
         out_specs=vmem,
         out_shape=pltpu.VMEM((parts, 3, rows, inner), BF16),
@@ -265,10 +277,15 @@
         on_chip(returned.reshape(2, heads, hd, hd)),
     )
     moved = lax.all_to_all(
-        grads.reshape(parts, 3 * rows, inner), "head", split_axis=0, concat_axis=0, tiled=True
+        grads.reshape(parts, 3 * rows, inner),
+        "head",
+        split_axis=0,
+        concat_axis=0,
+        axis_index_groups=[[(lead + p) % parts for p in range(parts)]],
+        tiled=True,
     ).reshape(parts, 3, rows, inner)
     return pl.pallas_call(
-        spread_kernel,
+        functools.partial(spread_kernel, lead),
         in_specs=[pl.BlockSpec(memory_space=pl.ANY)],
         out_specs=[pl.BlockSpec(memory_space=pl.ANY)] * 3,
         out_shape=[jax.ShapeDtypeStruct((rows, parts * inner), BF16)] * 3,

time: 129 us -> 127 us (0.984)
  the two profiles are of different devices: /device:TPU:32 before, /device:TPU:1 now
where the time goes in v3:
time: 127 us; the launch traced here: 126 us
  blocking collectives  96.7 us (76%)
  Pallas kernels  14.2 us (11%)
  starting transfers between devices  10.4 us (8%)
  waiting for transfers between devices  4.41 us (3%)
    all_to_all x1, blocking collectives, body(): lax.all_to_all(grads.reshape(parts, 3 * rows, inner), 'head', split_axis=...  84.2 us
    all_to_all x1, blocking collectives, body(): lax.all_to_all(scanned, 'seq', split_axis=0, concat_axis=0, tiled=True)  12.5 us
    all_to_all x1, starting transfers between devices, body(): lax.all_to_all(summary.reshape(blocks, piece, hd), 'seq', split_axis=0, c...  10.4 us
    pallas_call x1, Pallas kernels, body(): pl.pallas_call(functools.partial(local_kernel, length, docs, heads, block...  7.13 us
    all_to_all x1, waiting for transfers between devices, body(): lax.all_to_all(summary.reshape(blocks, piece, hd), 'seq', split_axis=0, c...  4.41 us
    pallas_call x1, Pallas kernels, body(): pl.pallas_call(functools.partial(summary_kernel, length, docs, heads), in...  2.75 us
    pallas_call x1, Pallas kernels, body(): pl.pallas_call(functools.partial(final_kernel, length, docs, heads, lead)...  2.69 us
  transfers between devices with their start and end apart: 1, of which 1 were waited for; matrix products, arithmetic and copies ran while one was open for 0% of the time, Pallas kernels for 6%

profile of v3, /device:TPU:1, one launch (start us, length us, event | category | flops | bytes accessed | tf_op | source)
XLA Modules:
  0.0 126.4 jit_solution(7838121643139458571)
XLA Ops:
  0.6 2.8 %summary.1 = f32[2,4,128,128]{3,2,1,0:T(8,128)} custom-call(f32[4]{0:T(128)} %rates_hbm.3, s32[8]{0:T(128)} %docs_hbm.3, bf16[512,512]{1,0:T(8,128)(2,1)} %k_hbm.3, bf16[512,512]{1,0:T(8,128)(2,1)} %v_hbm.3, bf16[512,512]{1,0:T(8,128)(2,1)} %q_hbm.1, bf16[512,512]{1,0:T(8,128)(2,1)} %g_hbm.3), custom_call_target="tpu_custom_call" | custom-call | tf_op jit(solution)/shard_map/summary/pallas_call | solution.py:225
  3.4 10.4 %all-to-all-start = ((f32[32,32,128]{2,1,0:T(8,128)}), f32[32,32,128]{2,1,0:T(8,128)S(1)}, u32[]{:S(2)}, u32[]{:S(2)}) async-start(f32[32,32,128]{2,1,0:T(8,128)} %bitcast), calls=%async_computation | async-start | bytes 1048576 | tf_op jit(solution)/shard_map/all_to_all | solution.py:239
  13.8 7.1 %local.1 = (f32[512,512]{1,0:T(8,128)}, f32[512,512]{1,0:T(8,128)}, f32[512,512]{1,0:T(8,128)}, f32[32,128]{1,0:T(8,128)S(1)}) custom-call(f32[4]{0:T(128)} %rates_hbm.3, s32[8]{0:T(128)} %docs_hbm.3, bf16[512,512]{1,0:T(8,128)(2,1)} %q_hbm.1, bf16[512,512]{1,0:T(8,128)(2,1)} %k_hbm.3, bf16[512,512]{1,0:T(8,128)(2,1)} %v_hbm.3, bf16[512,512]{1,0:T(8,128)(2,1)} %g_hbm.3), custom_call_target="tpu_custom_call" | custom-call | tf_op jit(solution)/shard_map/local/pallas_call | solution.py:242
  20.9 4.4 %all-to-all-done.in_ref = f32[32,32,128]{2,1,0:T(8,128)S(1)} async-done(((f32[32,32,128]{2,1,0:T(8,128)}), f32[32,32,128]{2,1,0:T(8,128)S(1)}, u32[]{:S(2)}, u32[]{:S(2)}) %all-to-all-start) | async-done | bytes 524320 | tf_op jit(solution)/shard_map/all_to_all | solution.py:239
  25.3 0.1 scan.1
  25.4 12.5 %all_to_all.15 = bf16[32,32,128]{2,1,0:T(8,128)(2,1)S(1)} all-to-all(bf16[32,32,128]{2,1,0:T(8,128)(2,1)S(1)} %scan.1), channel_id=1, replica_groups=mesh['seq'=32,'head'=16] {'seq'}, dimensions={0} | all-to-all | bytes 524288 | tf_op jit(solution)/shard_map/all_to_all | solution.py:260
  37.9 2.7 %final.1 = bf16[16,3,32,512]{3,2,1,0:T(8,128)(2,1)S(1)} custom-call(f32[4]{0:T(128)} %rates_hbm.3, s32[8]{0:T(128)} %docs_hbm.3, bf16[512,512]{1,0:T(8,128)(2,1)} %g_hbm.3, bf16[512,512]{1,0:T(8,128)(2,1)} %v_hbm.3, bf16[512,512]{1,0:T(8,128)(2,1)} %k_hbm.3, f32[512,512]{1,0:T(8,128)} %get-tuple-element.7.lq_hbm, f32[512,512]{1,0:T(8,128)} %get-tuple-element.8.lk_hbm, ...), custom_call_target="tpu_custom_call" | custom-call | tf_op jit(solution)/shard_map/final/pallas_call | solution.py:261
  40.6 84.2 %all_to_all.16 = bf16[16,96,512]{2,1,0:T(8,128)(2,1)S(1)} all-to-all(bf16[16,96,512]{2,1,0:T(8,128)(2,1)S(1)} %bitcast.5), channel_id=1, replica_groups={{11,12,13,14,15,0,1,2,3,4,5,6,7,8,9,10},{27,28,29,30,31,16,17,18,19,20,..., dimensions={0} | all-to-all | bytes 3145728 | tf_op jit(solution)/shard_map/all_to_all | solution.py:279
  124.9 1.5 %spread.1 = (bf16[32,8192]{1,0:T(8,128)(2,1)}, bf16[32,8192]{1,0:T(8,128)(2,1)}, bf16[32,8192]{1,0:T(8,128)(2,1)}) custom-call(bf16[16,3,32,512]{3,2,1,0:T(8,128)(2,1)S(1)} %bitcast.4), custom_call_target="tpu_custom_call" | custom-call | tf_op jit(solution)/shard_map/spread/pallas_call | solution.py:287
Async XLA Ops:
  3.4 21.9 %all-to-all-start = ((f32[32,32,128]{2,1,0:T(8,128)}), f32[32,32,128]{2,1,0:T(8,128)S(1)}, u32[]{:S(2)}, u32[]{:S(2)}) async-start(f32[32,32,128]{2,1,0:T(8,128)} %bitcast), calls=%async_computation | async-start | bytes 1048576 | tf_op jit(solution)/shard_map/all_to_all | solution.py:239

commit v4 on v3

--- a/solution.py
+++ b/solution.py
@@ -145,14 +145,14 @@
 
 def final_kernel(
     length, docs, heads, lead,
-    rates_hbm, docs_hbm, g_hbm, v_hbm, k_hbm, lq_hbm, lk_hbm, lv_hbm, s_ref, out_ref,
-    rates_ref, docs_ref, held, local, factors, sems,
+    rates_hbm, docs_hbm, lq_hbm, lk_hbm, lv_hbm, g_ref, v_ref, k_ref, s_ref, out_ref,
+    rates_ref, docs_ref, local, factors, sems,
 ):
     parts, _, rows, _ = out_ref.shape
     hd = s_ref.shape[-1]
     copies = fetch(
-        (docs_hbm, rates_hbm, g_hbm, lq_hbm, v_hbm, lk_hbm, k_hbm, lv_hbm),
-        (docs_ref, rates_ref) + sum(((held.at[i], local.at[i]) for i in range(3)), ()),
+        (docs_hbm, rates_hbm, lq_hbm, lk_hbm, lv_hbm),
+        (docs_ref, rates_ref, *(local.at[i] for i in range(3))),
         sems,
     )
     start_all(copies)
@@ -176,13 +176,12 @@
             far = jnp.exp(jnp.full((1, hd), -rate * (length - group - low), F32))
             factors[1, h, these] = jnp.where(row >= from_here - low, behind * far, 0.0)
 
-    for i in range(3):
-        copies[2 + 2 * i].wait()
-        copies[3 + 2 * i].wait()
+    for i, rows_ref in enumerate((g_ref, v_ref, k_ref)):
+        copies[2 + i].wait()
         for h in range(heads):
             at = slice(h * hd, (h + 1) * hd)
             matrix = s_ref[min(i, 1), h]
-            outer = dot(held[i, :, at], matrix, 1, 0 if i == 2 else 1)
+            outer = dot(rows_ref[:, at], matrix, 1, 0 if i == 2 else 1)
             grad = (local[i, :, at] + outer * factors[min(i, 1), h]).astype(BF16)
             grad = grad.reshape(parts, rows, hd)
             out_ref[: parts - lead, i, :, at] = grad[lead:]
@@ -260,20 +259,20 @@
     returned = lax.all_to_all(scanned, "seq", split_axis=0, concat_axis=0, tiled=True)
     grads = pl.pallas_call(
         functools.partial(final_kernel, length, docs, heads, lead),
-        in_specs=[anywhere] * 8 + [vmem],
+        in_specs=[anywhere] * 5 + [vmem] * 4,
         out_specs=vmem,
         out_shape=pltpu.VMEM((parts, 3, rows, inner), BF16),
         scratch_shapes=[
             pltpu.SMEM((heads,), F32),
             pltpu.SMEM((docs,), jnp.int32),
-            pltpu.VMEM((3, length, inner), BF16),
             pltpu.VMEM((3, length, inner), F32),
             pltpu.VMEM((2, heads, length, hd), F32),
-            pltpu.SemaphoreType.DMA((8,)),
+            pltpu.SemaphoreType.DMA((5,)),
         ],
         name="final",
     )(
-        rates, doc_lengths, grad_out, values, keys, *local,
+        rates, doc_lengths, *local,
+        *[on_chip(a) for a in (grad_out, values, keys)],
         on_chip(returned.reshape(2, heads, hd, hd)),
     )
     moved = lax.all_to_all(

time: 127 us -> 126 us (level)
  no operation moved by 1% of the time
where the time goes in v4:
time: 126 us
  blocking collectives  96.7 us (77%)
  Pallas kernels  13.8 us (11%)
  starting transfers between devices  10.4 us (8%)
  waiting for transfers between devices  4.29 us (3%)
    all_to_all x1, blocking collectives, body(): lax.all_to_all(grads.reshape(parts, 3 * rows, inner), 'head', split_axis=...  84.2 us
    all_to_all x1, blocking collectives, body(): lax.all_to_all(scanned, 'seq', split_axis=0, concat_axis=0, tiled=True)  12.5 us
    all_to_all x1, starting transfers between devices, body(): lax.all_to_all(summary.reshape(blocks, piece, hd), 'seq', split_axis=0, c...  10.4 us
    pallas_call x1, Pallas kernels, body(): pl.pallas_call(functools.partial(local_kernel, length, docs, heads, block...  7.22 us
    all_to_all x1, waiting for transfers between devices, body(): lax.all_to_all(summary.reshape(blocks, piece, hd), 'seq', split_axis=0, c...  4.29 us
    pallas_call x1, Pallas kernels, body(): pl.pallas_call(functools.partial(summary_kernel, length, docs, heads), in...  2.75 us
  transfers between devices with their start and end apart: 1, of which 1 were waited for; matrix products, arithmetic and copies ran while one was open for 0% of the time, Pallas kernels for 6%

profile of v4, /device:TPU:1, one launch (start us, length us, event | category | flops | bytes accessed | tf_op | source)
XLA Modules:
  0.0 125.9 jit_solution(14223067042687154451)
XLA Ops:
  0.6 2.8 %summary.1 = f32[2,4,128,128]{3,2,1,0:T(8,128)} custom-call(f32[4]{0:T(128)} %rates_hbm.3, s32[8]{0:T(128)} %docs_hbm.3, bf16[512,512]{1,0:T(8,128)(2,1)} %k_ref.3, bf16[512,512]{1,0:T(8,128)(2,1)} %v_ref.3, bf16[512,512]{1,0:T(8,128)(2,1)} %q_hbm.1, bf16[512,512]{1,0:T(8,128)(2,1)} %g_ref.3), custom_call_target="tpu_custom_call" | custom-call | tf_op jit(solution)/shard_map/summary/pallas_call | solution.py:224
  3.4 10.4 %all-to-all-start = ((f32[32,32,128]{2,1,0:T(8,128)}), f32[32,32,128]{2,1,0:T(8,128)S(1)}, u32[]{:S(2)}, u32[]{:S(2)}) async-start(f32[32,32,128]{2,1,0:T(8,128)} %bitcast), calls=%async_computation | async-start | bytes 1048576 | tf_op jit(solution)/shard_map/all_to_all | solution.py:238
  13.8 0.0 copy-start.1
  13.8 0.0 copy-start.2
  13.8 7.2 %local.1 = (f32[512,512]{1,0:T(8,128)}, f32[512,512]{1,0:T(8,128)}, f32[512,512]{1,0:T(8,128)}, f32[32,128]{1,0:T(8,128)S(1)}) custom-call(f32[4]{0:T(128)} %rates_hbm.3, s32[8]{0:T(128)} %docs_hbm.3, bf16[512,512]{1,0:T(8,128)(2,1)} %q_hbm.1, bf16[512,512]{1,0:T(8,128)(2,1)} %k_ref.3, bf16[512,512]{1,0:T(8,128)(2,1)} %v_ref.3, bf16[512,512]{1,0:T(8,128)(2,1)} %g_ref.3), custom_call_target="tpu_custom_call" | custom-call | tf_op jit(solution)/shard_map/local/pallas_call | solution.py:241
  21.0 0.0 copy-start
  21.0 4.3 %all-to-all-done.in_ref = f32[32,32,128]{2,1,0:T(8,128)S(1)} async-done(((f32[32,32,128]{2,1,0:T(8,128)}), f32[32,32,128]{2,1,0:T(8,128)S(1)}, u32[]{:S(2)}, u32[]{:S(2)}) %all-to-all-start) | async-done | bytes 524320 | tf_op jit(solution)/shard_map/all_to_all | solution.py:238
  25.3 0.1 scan.1
  25.4 12.5 %all_to_all.15 = bf16[32,32,128]{2,1,0:T(8,128)(2,1)S(1)} all-to-all(bf16[32,32,128]{2,1,0:T(8,128)(2,1)S(1)} %scan.1), channel_id=1, replica_groups=mesh['seq'=32,'head'=16] {'seq'}, dimensions={0} | all-to-all | bytes 524288 | tf_op jit(solution)/shard_map/all_to_all | solution.py:259
  37.9 0.0 copy-done.1
  37.9 0.0 copy-done.2
  37.9 0.0 copy-done
  37.9 2.2 %final.1 = bf16[16,3,32,512]{3,2,1,0:T(8,128)(2,1)S(1)} custom-call(f32[4]{0:T(128)} %rates_hbm.3, s32[8]{0:T(128)} %docs_hbm.3, f32[512,512]{1,0:T(8,128)} %get-tuple-element.7.lq_hbm, f32[512,512]{1,0:T(8,128)} %get-tuple-element.8.lk_hbm, f32[512,512]{1,0:T(8,128)} %get-tuple-element.9.lv_hbm, bf16[512,512]{1,0:T(8,128)(2,1)S(1)} %copy-done.2, ...), custom_call_target="tpu_custom_call" | custom-call | tf_op jit(solution)/shard_map/final/pallas_call | solution.py:260
  40.1 84.2 %all_to_all.16 = bf16[16,96,512]{2,1,0:T(8,128)(2,1)S(1)} all-to-all(bf16[16,96,512]{2,1,0:T(8,128)(2,1)S(1)} %bitcast.5), channel_id=1, replica_groups={{11,12,13,14,15,0,1,2,3,4,5,6,7,8,9,10},{27,28,29,30,31,16,17,18,19,20,..., dimensions={0} | all-to-all | bytes 3145728 | tf_op jit(solution)/shard_map/all_to_all | solution.py:278
  124.4 1.5 %spread.1 = (bf16[32,8192]{1,0:T(8,128)(2,1)}, bf16[32,8192]{1,0:T(8,128)(2,1)}, bf16[32,8192]{1,0:T(8,128)(2,1)}) custom-call(bf16[16,3,32,512]{3,2,1,0:T(8,128)(2,1)S(1)} %bitcast.4), custom_call_target="tpu_custom_call" | custom-call | tf_op jit(solution)/shard_map/spread/pallas_call | solution.py:286
Async XLA Ops:
  3.4 21.9 %all-to-all-start = ((f32[32,32,128]{2,1,0:T(8,128)}), f32[32,32,128]{2,1,0:T(8,128)S(1)}, u32[]{:S(2)}, u32[]{:S(2)}) async-start(f32[32,32,128]{2,1,0:T(8,128)} %bitcast), calls=%async_computation | async-start | bytes 1048576 | tf_op jit(solution)/shard_map/all_to_all | solution.py:238
  13.8 24.1 %copy-start.1 = (bf16[512,512]{1,0:T(8,128)(2,1)S(1)}, bf16[512,512]{1,0:T(8,128)(2,1)}, u32[]{:S(2)}) copy-start(bf16[512,512]{1,0:T(8,128)(2,1)} %v_ref.3) | copy-start | bytes 1572868
  13.8 24.1 %copy-start.2 = (bf16[512,512]{1,0:T(8,128)(2,1)S(1)}, bf16[512,512]{1,0:T(8,128)(2,1)}, u32[]{:S(2)}) copy-start(bf16[512,512]{1,0:T(8,128)(2,1)} %g_ref.3) | copy-start | bytes 1572868
  21.0 16.9 %copy-start = (bf16[512,512]{1,0:T(8,128)(2,1)S(1)}, bf16[512,512]{1,0:T(8,128)(2,1)}, u32[]{:S(2)}) copy-start(bf16[512,512]{1,0:T(8,128)(2,1)} %k_ref.3) | copy-start | bytes 1572868

commit v5 on v4

--- a/solution.py
+++ b/solution.py
@@ -190,16 +190,20 @@
 
 def spread_kernel(lead, in_ref, *refs):
     outs, sems = refs[:3], refs[3]
-    parts, _, _, width = in_ref.shape
+    parts, _, tiles, _, _ = in_ref.shape
     copies = []
     for i in range(3):
-        for h in range(parts):
-            column = (h + lead) % parts * width
-            copy = pltpu.make_async_copy(
-                in_ref.at[h, i], outs[i].at[:, pl.ds(column, width)], sems.at[i, h]
-            )
-            copy.start()
-            copies.append(copy)
+        for r in range(tiles):
+            for side, (low, size, to) in enumerate(
+                ((0, parts - lead, lead), (parts - lead, lead, 0))
+            ):
+                copy = pltpu.make_async_copy(
+                    in_ref.at[pl.ds(low, size), i, r],
+                    outs[i].at[r, pl.ds(to, size)],
+                    sems.at[i, r, side],
+                )
+                copy.start()
+                copies.append(copy)
     for copy in copies:
         copy.wait()
 
@@ -282,16 +286,17 @@
         concat_axis=0,
         axis_index_groups=[[(lead + p) % parts for p in range(parts)]],
         tiled=True,
-    ).reshape(parts, 3, rows, inner)
-    return pl.pallas_call(
+    ).reshape(parts, 3, rows // 8, 8, inner)
+    spread = pl.pallas_call(
         functools.partial(spread_kernel, lead),
-        in_specs=[pl.BlockSpec(memory_space=pl.ANY)],
-        out_specs=[pl.BlockSpec(memory_space=pl.ANY)] * 3,
-        out_shape=[jax.ShapeDtypeStruct((rows, parts * inner), BF16)] * 3,
-        scratch_shapes=[pltpu.SemaphoreType.DMA((3, parts))],
+        in_specs=[anywhere],
+        out_specs=[anywhere] * 3,
+        out_shape=[jax.ShapeDtypeStruct((rows // 8, parts, 8, inner), BF16)] * 3,
+        scratch_shapes=[pltpu.SemaphoreType.DMA((3, rows // 8, 2))],
         compiler_params=pltpu.CompilerParams(vmem_limit_bytes=4 << 20),
         name="spread",
     )(moved)
+    return tuple(a.transpose(0, 2, 1, 3).reshape(rows, parts * inner) for a in spread)
 
 
 def solution(mesh):

time: 126 us -> 126 us (level)
  no operation moved by 1% of the time
where the time goes in v5:
time: 126 us
  blocking collectives  96.7 us (77%)
  Pallas kernels  13.6 us (11%)
  starting transfers between devices  10.4 us (8%)
  waiting for transfers between devices  4.29 us (3%)
    all_to_all x1, blocking collectives, body(): lax.all_to_all(grads.reshape(parts, 3 * rows, inner), 'head', split_axis=...  84.2 us
    all_to_all x1, blocking collectives, body(): lax.all_to_all(scanned, 'seq', split_axis=0, concat_axis=0, tiled=True)  12.5 us
    all_to_all x1, starting transfers between devices, body(): lax.all_to_all(summary.reshape(blocks, piece, hd), 'seq', split_axis=0, c...  10.4 us
    pallas_call x1, Pallas kernels, body(): pl.pallas_call(functools.partial(local_kernel, length, docs, heads, block...  7.22 us
    all_to_all x1, waiting for transfers between devices, body(): lax.all_to_all(summary.reshape(blocks, piece, hd), 'seq', split_axis=0, c...  4.29 us
    pallas_call x1, Pallas kernels, body(): pl.pallas_call(functools.partial(summary_kernel, length, docs, heads), in...  2.75 us
  transfers between devices with their start and end apart: 1, of which 1 were waited for; matrix products, arithmetic and copies ran while one was open for 0% of the time, Pallas kernels for 6%

profile of v5, /device:TPU:1, one launch (start us, length us, event | category | flops | bytes accessed | tf_op | source)
XLA Modules:
  0.0 125.7 jit_solution(11343030495232898380)
XLA Ops:
  0.6 2.8 %summary.1 = f32[2,4,128,128]{3,2,1,0:T(8,128)} custom-call(f32[4]{0:T(128)} %rates_hbm.3, s32[8]{0:T(128)} %docs_hbm.3, bf16[512,512]{1,0:T(8,128)(2,1)} %k_ref.3, bf16[512,512]{1,0:T(8,128)(2,1)} %v_ref.3, bf16[512,512]{1,0:T(8,128)(2,1)} %q_hbm.1, bf16[512,512]{1,0:T(8,128)(2,1)} %g_ref.3), custom_call_target="tpu_custom_call" | custom-call | tf_op jit(solution)/shard_map/summary/pallas_call | solution.py:228
  3.4 10.4 %all-to-all-start = ((f32[32,32,128]{2,1,0:T(8,128)}), f32[32,32,128]{2,1,0:T(8,128)S(1)}, u32[]{:S(2)}, u32[]{:S(2)}) async-start(f32[32,32,128]{2,1,0:T(8,128)} %bitcast), calls=%async_computation | async-start | bytes 1048576 | tf_op jit(solution)/shard_map/all_to_all | solution.py:242
  13.8 0.0 copy-start.1
  13.8 0.0 copy-start.2
  13.8 7.2 %local.1 = (f32[512,512]{1,0:T(8,128)}, f32[512,512]{1,0:T(8,128)}, f32[512,512]{1,0:T(8,128)}, f32[32,128]{1,0:T(8,128)S(1)}) custom-call(f32[4]{0:T(128)} %rates_hbm.3, s32[8]{0:T(128)} %docs_hbm.3, bf16[512,512]{1,0:T(8,128)(2,1)} %q_hbm.1, bf16[512,512]{1,0:T(8,128)(2,1)} %k_ref.3, bf16[512,512]{1,0:T(8,128)(2,1)} %v_ref.3, bf16[512,512]{1,0:T(8,128)(2,1)} %g_ref.3), custom_call_target="tpu_custom_call" | custom-call | tf_op jit(solution)/shard_map/local/pallas_call | solution.py:245
  21.0 0.0 copy-start
  21.0 4.3 %all-to-all-done.in_ref = f32[32,32,128]{2,1,0:T(8,128)S(1)} async-done(((f32[32,32,128]{2,1,0:T(8,128)}), f32[32,32,128]{2,1,0:T(8,128)S(1)}, u32[]{:S(2)}, u32[]{:S(2)}) %all-to-all-start) | async-done | bytes 524320 | tf_op jit(solution)/shard_map/all_to_all | solution.py:242
  25.3 0.1 scan.1
  25.4 12.5 %all_to_all.15 = bf16[32,32,128]{2,1,0:T(8,128)(2,1)S(1)} all-to-all(bf16[32,32,128]{2,1,0:T(8,128)(2,1)S(1)} %scan.1), channel_id=1, replica_groups=mesh['seq'=32,'head'=16] {'seq'}, dimensions={0} | all-to-all | bytes 524288 | tf_op jit(solution)/shard_map/all_to_all | solution.py:263
  37.9 0.0 copy-done.1
  37.9 0.0 copy-done.2
  37.9 0.0 copy-done
  37.9 2.2 %final.1 = bf16[16,3,32,512]{3,2,1,0:T(8,128)(2,1)S(1)} custom-call(f32[4]{0:T(128)} %rates_hbm.3, s32[8]{0:T(128)} %docs_hbm.3, f32[512,512]{1,0:T(8,128)} %get-tuple-element.10.lq_hbm, f32[512,512]{1,0:T(8,128)} %get-tuple-element.11.lk_hbm, f32[512,512]{1,0:T(8,128)} %get-tuple-element.12.lv_hbm, bf16[512,512]{1,0:T(8,128)(2,1)S(1)} %copy-done.2, ...), custom_call_target="tpu_custom_call" | custom-call | tf_op jit(solution)/shard_map/final/pallas_call | solution.py:264
  40.1 84.2 %all_to_all.16 = bf16[16,96,512]{2,1,0:T(8,128)(2,1)S(1)} all-to-all(bf16[16,96,512]{2,1,0:T(8,128)(2,1)S(1)} %bitcast.14), channel_id=1, replica_groups={{11,12,13,14,15,0,1,2,3,4,5,6,7,8,9,10},{27,28,29,30,31,16,17,18,19,20,..., dimensions={0} | all-to-all | bytes 3145728 | tf_op jit(solution)/shard_map/all_to_all | solution.py:282
  124.4 1.3 %spread.1 = (bf16[4,16,8,512]{3,2,1,0:T(8,128)(2,1)}, bf16[4,16,8,512]{3,2,1,0:T(8,128)(2,1)}, bf16[4,16,8,512]{3,2,1,0:T(8,128)(2,1)}) custom-call(bf16[16,3,4,8,512]{4,3,2,1,0:T(8,128)(2,1)S(1)} %bitcast.13), custom_call_target="tpu_custom_call" | custom-call | tf_op jit(solution)/shard_map/spread/pallas_call | solution.py:290
Async XLA Ops:
  3.4 21.9 %all-to-all-start = ((f32[32,32,128]{2,1,0:T(8,128)}), f32[32,32,128]{2,1,0:T(8,128)S(1)}, u32[]{:S(2)}, u32[]{:S(2)}) async-start(f32[32,32,128]{2,1,0:T(8,128)} %bitcast), calls=%async_computation | async-start | bytes 1048576 | tf_op jit(solution)/shard_map/all_to_all | solution.py:242
  13.8 24.1 %copy-start.1 = (bf16[512,512]{1,0:T(8,128)(2,1)S(1)}, bf16[512,512]{1,0:T(8,128)(2,1)}, u32[]{:S(2)}) copy-start(bf16[512,512]{1,0:T(8,128)(2,1)} %v_ref.3) | copy-start | bytes 1572868
  13.8 24.1 %copy-start.2 = (bf16[512,512]{1,0:T(8,128)(2,1)S(1)}, bf16[512,512]{1,0:T(8,128)(2,1)}, u32[]{:S(2)}) copy-start(bf16[512,512]{1,0:T(8,128)(2,1)} %g_ref.3) | copy-start | bytes 1572868
  21.0 16.9 %copy-start = (bf16[512,512]{1,0:T(8,128)(2,1)S(1)}, bf16[512,512]{1,0:T(8,128)(2,1)}, u32[]{:S(2)}) copy-start(bf16[512,512]{1,0:T(8,128)(2,1)} %k_ref.3) | copy-start | bytes 1572868
